TPU v7x, 32 devices: a whole 2x2x4 slice. The times are simulated.
32 devices in a mesh: block: 4 (over y, x), tok: 8 (over z, core).
Axes of the slice: x: 2, y: 2, z: 4, core: 2. Of those that a mesh axis runs over, the one named last changes fastest.
Arguments:
- queries: float32 [4096, 256], P(('block', 'tok')), may hold values from -6 to 6
- keys: float32 [4096, 256], P(('block', 'tok')), may hold values from -6 to 6
- values: float32 [4096, 256], P(('block', 'tok')), may hold values from -6 to 6
- rates: float32 [4096], P(('block', 'tok')), may hold values from 0.0001 to 0.001
- states: float32 [4, 3, 256, 256], P('block', None, 'tok'), may hold values from -0.375 to 0.375
- out_cot: float32 [4096, 256], P(('block', 'tok')), may hold values from -6 to 6
- final_cot: float32 [3, 256, 256], P(None, 'tok'), may hold values from -6 to 6
Outputs:
- d_queries: float32 [4096, 256], P(('block', 'tok'))
- d_keys: float32 [4096, 256], P(('block', 'tok'))
- d_values: float32 [4096, 256], P(('block', 'tok'))
- d_rates: float32 [4096], P(('block', 'tok'))
- d_states: float32 [4, 3, 256, 256], P('block', None, 'tok')
All inputs are finite; a program needn't handle non-finite values.
Results may differ from a plain program's by a relative error of at most 0.00029.
Values sent between devices are 32-bit elements; how exact they have to be, the bound alone decides.
No kernel may reach another device: no remote copies, remote signals or barrier semaphores. Data moves between devices by JAX's collectives and lax.ppermute only.
A program may use at most 64 MiB of HBM per device.

v0:
```python
import jax
import jax.numpy as jnp
from jax import lax
from jax.sharding import PartitionSpec as P

EPS = 1e-06
HIGH = lax.Precision.HIGHEST


def from_behind(array, axis, by):
    devices = lax.axis_size(axis)
    pairs = [(i, i + by) for i in range(devices) if 0 <= i + by < devices]
    return lax.ppermute(array, axis, pairs)


def apply_fast(weights, inputs):
    first = jnp.dot(inputs, weights[0], precision=HIGH, preferred_element_type=jnp.float32)
    gate = jnp.dot(inputs, weights[1], precision=HIGH, preferred_element_type=jnp.float32)
    mixed = jax.nn.silu(first) * gate
    return jnp.dot(mixed, weights[2], precision=HIGH, preferred_element_type=jnp.float32)


def update_grad(weights, keys, values, rates):

    def loss(current):
        return -jnp.sum(rates[:, None] * apply_fast(current, keys) * values)

    return jax.grad(loss)(weights)


def norm_adjoint(incoming, shifted, own, row_norm, new_norm):
    inner = jnp.sum(incoming * shifted, axis=-1, keepdims=True)
    d_shifted = (
        row_norm / new_norm * incoming
        - row_norm * inner / (new_norm * new_norm * new_norm) * shifted
    )
    direct = d_shifted + inner / new_norm * own / row_norm
    return (d_shifted, direct)


def per_device(queries, keys, values, rates, states, out_cot, final_cot):
    groups = lax.axis_size("block")
    position = lax.axis_index("block")
    own_rows = states[0]
    gathered = lax.all_gather(own_rows, "tok", axis=1, tiled=True)
    _, apply_back = jax.vjp(apply_fast, gathered, queries)
    apply_state, d_queries = apply_back(out_cot)
    grad_part, second_back = jax.vjp(update_grad, gathered, keys, values, rates)
    grad_rows = lax.psum_scatter(grad_part, "tok", scatter_dimension=1, tiled=True)
    shifted = own_rows - grad_rows
    row_norm = jnp.sqrt(jnp.sum(own_rows * own_rows, axis=-1, keepdims=True) + EPS)
    new_norm = jnp.sqrt(jnp.sum(shifted * shifted, axis=-1, keepdims=True) + EPS)
    zero_back = (
        jnp.zeros_like(gathered),
        jnp.zeros_like(keys),
        jnp.zeros_like(values),
        jnp.zeros_like(rates),
    )
    incoming = final_cot
    d_keys = jnp.zeros_like(keys)
    d_values = jnp.zeros_like(values)
    d_rates = jnp.zeros_like(rates)
    d_rows = jnp.zeros_like(own_rows)
    for section in range(groups):
        active = position == groups - 1 - section
        d_shifted, direct = norm_adjoint(incoming, shifted, own_rows, row_norm, new_norm)
        d_grad = lax.all_gather(-d_shifted, "tok", axis=1, tiled=True)
        second_state, second_keys, second_values, second_rates = lax.cond(
            active, lambda cot: second_back(cot), lambda cot: zero_back, d_grad
        )
        summed = lax.psum_scatter(
            second_state + apply_state, "tok", scatter_dimension=1, tiled=True
        )
        rows_now = summed + direct
        d_keys = jnp.where(active, second_keys, d_keys)
        d_values = jnp.where(active, second_values, d_values)
        d_rates = jnp.where(active, second_rates, d_rates)
        d_rows = jnp.where(active, rows_now, d_rows)
        if section + 1 < groups:
            incoming = from_behind(rows_now, "block", -1)
    return (d_queries, d_keys, d_values, d_rates, d_rows[None])


def solution(mesh):
    return jax.shard_map(
        per_device,
        mesh=mesh,
        in_specs=(
            P(("block", "tok"), None),
            P(("block", "tok"), None),
            P(("block", "tok"), None),
            P(("block", "tok")),
            P("block", None, "tok", None),
            P(("block", "tok"), None),
            P(None, "tok", None),
        ),
        out_specs=(
            P(("block", "tok"), None),
            P(("block", "tok"), None),
            P(("block", "tok"), None),
            P(("block", "tok")),
            P("block", None, "tok", None),
        ),
        check_vma=False,
    )
```

profile of v0, /device:TPU:0, one launch (start us, length us, event | category | flops | bytes accessed | tf_op | source)
XLA Modules:
  0.0 317.6 jit_solution(9422228278440571591)
XLA Ops:
  7.9 17.5 %all-gather = f32[1,3,256,256]{3,2,1,0:T(8,128)S(1)} all-gather(f32[1,3,32,256]{3,2,1,0:T(8,128)} %param.19), channel_id=2, replica_groups=mesh['block'=4,'tok'=8] {'tok'}, dimensions={2}, use_global_device_ids=true | all-gather | bytes 884736 | tf_op jit(solution)/shard_map/all_gather | solution.py:45
  34.6 29.1 %reduce-scatter.6.cloned.1.call-done = f32[3,32,256]{2,1,0:T(8,128)} async-done(((f32[3,256,256]{2,1,0:T(8,128)}), f32[3,32,256]{2,1,0:T(8,128)}) %reduce-scatter.6.cloned.1.call-update) | async-done | bytes 98320 | tf_op jit(solution)/shard_map/reduce_scatter | solution.py:49
  65.0 15.9 %all_gather.16 = f32[3,256,256]{2,1,0:T(8,128)S(1)} all-gather(f32[3,32,256]{2,1,0:T(8,128)S(1)} %fusion.92), channel_id=1, replica_groups=mesh['block'=4,'tok'=8] {'tok'}, dimensions={1}, use_global_device_ids=true | all-gather | bytes 884736 | tf_op jit(solution)/shard_map/all_gather | solution.py:67
  81.5 1.4 conditional.4
  83.9 35.0 %reduce-scatter.8.cloned.1.call-done = f32[3,32,256]{2,1,0:T(8,128)} async-done(((f32[3,256,256]{2,1,0:T(8,128)}), f32[3,32,256]{2,1,0:T(8,128)}) %reduce-scatter.8.cloned.1.call-update) | async-done | bytes 98320 | tf_op jit(solution)/shard_map/reduce_scatter | solution.py:71
  118.9 1.7 fusion.76
  120.6 1.3 collective-permute-start
  121.9 5.5 %collective-permute-done = f32[3,32,256]{2,1,0:T(8,128)} collective-permute-done((f32[3,32,256]{2,1,0:T(8,128)}, f32[3,32,256]{2,1,0:T(8,128)}, u32[]{:S(2)}, u32[]{:S(2)}) %collective-permute-start) | collective-permute-done | bytes 98336 | tf_op jit(solution)/shard_map/ppermute | solution.py:13
  129.6 15.8 %all_gather.17 = f32[3,256,256]{2,1,0:T(8,128)S(1)} all-gather(f32[3,32,256]{2,1,0:T(8,128)S(1)} %fusion.93), channel_id=1, replica_groups=mesh['block'=4,'tok'=8] {'tok'}, dimensions={1}, use_global_device_ids=true | all-gather | bytes 884736 | tf_op jit(solution)/shard_map/all_gather | solution.py:67
  145.4 1.6 conditional.5
  148.1 34.5 %reduce-scatter.10.cloned.1.call-done = f32[3,32,256]{2,1,0:T(8,128)} async-done(((f32[3,256,256]{2,1,0:T(8,128)}), f32[3,32,256]{2,1,0:T(8,128)}) %reduce-scatter.10.cloned.1.call-update) | async-done | bytes 98320 | tf_op jit(solution)/shard_map/reduce_scatter | solution.py:71
  182.6 1.7 fusion.79
  184.3 1.3 collective-permute-start.1
  185.6 5.5 %collective-permute-done.1 = f32[3,32,256]{2,1,0:T(8,128)} collective-permute-done((f32[3,32,256]{2,1,0:T(8,128)}, f32[3,32,256]{2,1,0:T(8,128)}, u32[]{:S(2)}, u32[]{:S(2)}) %collective-permute-start.1) | collective-permute-done | bytes 98336 | tf_op jit(solution)/shard_map/ppermute | solution.py:13
  193.2 15.8 %all_gather.18 = f32[3,256,256]{2,1,0:T(8,128)S(1)} all-gather(f32[3,32,256]{2,1,0:T(8,128)S(1)} %fusion.94), channel_id=1, replica_groups=mesh['block'=4,'tok'=8] {'tok'}, dimensions={1}, use_global_device_ids=true | all-gather | bytes 884736 | tf_op jit(solution)/shard_map/all_gather | solution.py:67
  209.1 1.4 conditional.6
  211.5 35.1 %reduce-scatter.12.cloned.1.call-done = f32[3,32,256]{2,1,0:T(8,128)} async-done(((f32[3,256,256]{2,1,0:T(8,128)}), f32[3,32,256]{2,1,0:T(8,128)}) %reduce-scatter.12.cloned.1.call-update) | async-done | bytes 98320 | tf_op jit(solution)/shard_map/reduce_scatter | solution.py:71
  246.6 1.7 fusion.82
  249.6 5.5 %collective-permute-done.2 = f32[3,32,256]{2,1,0:T(8,128)} collective-permute-done((f32[3,32,256]{2,1,0:T(8,128)}, f32[3,32,256]{2,1,0:T(8,128)}, u32[]{:S(2)}, u32[]{:S(2)}) %collective-permute-start.2) | collective-permute-done | bytes 98336 | tf_op jit(solution)/shard_map/ppermute | solution.py:13
  257.3 15.8 %all_gather.19 = f32[3,256,256]{2,1,0:T(8,128)S(1)} all-gather(f32[3,32,256]{2,1,0:T(8,128)S(1)} %fusion.95), channel_id=1, replica_groups=mesh['block'=4,'tok'=8] {'tok'}, dimensions={1}, use_global_device_ids=true | all-gather | bytes 884736 | tf_op jit(solution)/shard_map/all_gather | solution.py:67
  273.1 6.2 %conditional.7 = (f32[3,256,256]{2,1,0:T(8,128)S(1)}, f32[128,256]{1,0:T(8,128)}, f32[128,256]{1,0:T(8,128)}, f32[128]{0:T(128)S(1)}) conditional(s32[]{:T(128)} %convert_element_type.12, () %tuple.51, (f32[3,256,256]{2,1,0:T(8,128)S(1)}, f32[128,256]{1,0:T(8,128)S(1)}, f32[128,256]{1,0:T(8,128)S(1)}, f32[128,256]{1,0:T(8,128)S(1)}, ...), branch_computations={%region_19.20_spmd, %region_20.22_spmd} | conditional | flops 1209499520 | bytes 10880032 | solution.py:68
  283.7 1.7 select_select_fusion
  285.4 23.9 %reduce-scatter.14.cloned.1.call-done = f32[3,32,256]{2,1,0:T(8,128)} async-done(((f32[3,256,256]{2,1,0:T(8,128)}), f32[3,32,256]{2,1,0:T(8,128)}) %reduce-scatter.14.cloned.1.call-update) | async-done | bytes 98320 | tf_op jit(solution)/shard_map/reduce_scatter | solution.py:71
  309.3 1.7 fusion.72
  (162 shorter events, 36.6 us)
Async XLA Ops:
  7.2 23.4 %copy-start = (f32[128,256]{1,0:T(8,128)S(1)}, f32[128,256]{1,0:T(8,128)}, u32[]{:S(2)}) copy-start(f32[128,256]{1,0:T(8,128)} %param.15) | copy-start | bytes 393220
  7.2 56.5 %reduce-scatter.6.cloned.1.call-start = ((), (), s32[]{:S(2)}) async-start(), calls=%async_computation.5 | async-start | bytes 884736 | tf_op jit(solution)/shard_map/reduce_scatter | solution.py:49
  7.9 17.6 %copy-start.43 = (f32[128,256]{1,0:T(8,128)S(1)}, f32[128,256]{1,0:T(8,128)}, u32[]{:S(2)}) copy-start(f32[128,256]{1,0:T(8,128)} %param.17) | copy-start | bytes 393220
  30.5 88.4 %reduce-scatter.8.cloned.1.call-start = ((), (), s32[]{:S(2)}) async-start(), calls=%async_computation.6 | async-start | bytes 884736 | tf_op jit(solution)/shard_map/reduce_scatter | solution.py:71
  33.7 30.0 %copy-start.20 = (f32[1,3,32,256]{3,2,1,0:T(8,128)S(1)}, f32[1,3,32,256]{3,2,1,0:T(8,128)}, u32[]{:S(2)}) copy-start(f32[1,3,32,256]{3,2,1,0:T(8,128)} %param.19) | copy-start | bytes 294916
  63.7 17.2 %copy-start.33 = (f32[128,256]{1,0:T(8,128)S(1)}, f32[128,256]{1,0:T(8,128)}, u32[]{:S(2)}) copy-start(f32[128,256]{1,0:T(8,128)} %get-tuple-element.291) | copy-start | bytes 393220
  83.9 98.7 %reduce-scatter.10.cloned.1.call-start = ((), (), s32[]{:S(2)}) async-start(), calls=%async_computation.7 | async-start | bytes 884736 | tf_op jit(solution)/shard_map/reduce_scatter | solution.py:71
  120.6 6.8 %collective-permute-start = (f32[3,32,256]{2,1,0:T(8,128)}, f32[3,32,256]{2,1,0:T(8,128)}, u32[]{:S(2)}, u32[]{:S(2)}) collective-permute-start(f32[3,32,256]{2,1,0:T(8,128)} %fusion.76), channel_id=1, source_target_pairs={{8,0},{16,8},{24,16},{9,1},{17,9},{25,17},{10,2},{18,10},{26,18},{... | collective-permute-start | bytes 294920 | tf_op jit(solution)/shard_map/ppermute | solution.py:13
  127.4 17.9 %copy-start.34 = (f32[128,256]{1,0:T(8,128)S(1)}, f32[128,256]{1,0:T(8,128)}, u32[]{:S(2)}) copy-start(f32[128,256]{1,0:T(8,128)} %get-tuple-element.291) | copy-start | bytes 393220
  128.5 16.9 %copy-start.22 = (f32[128,256]{1,0:T(8,128)S(1)}, f32[128,256]{1,0:T(8,128)}, u32[]{:S(2)}) copy-start(f32[128,256]{1,0:T(8,128)} %get-tuple-element.312) | copy-start | bytes 393220
  128.5 16.9 %copy-start.26 = (f32[128,256]{1,0:T(8,128)S(1)}, f32[128,256]{1,0:T(8,128)}, u32[]{:S(2)}) copy-start(f32[128,256]{1,0:T(8,128)} %get-tuple-element.314) | copy-start | bytes 393220
  128.5 16.9 %copy-start.30 = (f32[128,256]{1,0:T(8,128)S(1)}, f32[128,256]{1,0:T(8,128)}, u32[]{:S(2)}) copy-start(f32[128,256]{1,0:T(8,128)} %get-tuple-element.315) | copy-start | bytes 393220
  148.1 98.6 %reduce-scatter.12.cloned.1.call-start = ((), (), s32[]{:S(2)}) async-start(), calls=%async_computation.8 | async-start | bytes 884736 | tf_op jit(solution)/shard_map/reduce_scatter | solution.py:71
  184.3 6.8 %collective-permute-start.1 = (f32[3,32,256]{2,1,0:T(8,128)}, f32[3,32,256]{2,1,0:T(8,128)}, u32[]{:S(2)}, u32[]{:S(2)}) collective-permute-start(f32[3,32,256]{2,1,0:T(8,128)} %fusion.79), channel_id=1, source_target_pairs={{8,0},{16,8},{24,16},{9,1},{17,9},{25,17},{10,2},{18,10},{26,18},{... | collective-permute-start | bytes 294920 | tf_op jit(solution)/shard_map/ppermute | solution.py:13
  191.1 17.9 %copy-start.35 = (f32[128,256]{1,0:T(8,128)S(1)}, f32[128,256]{1,0:T(8,128)}, u32[]{:S(2)}) copy-start(f32[128,256]{1,0:T(8,128)} %get-tuple-element.291) | copy-start | bytes 393220
  192.1 16.9 %copy-start.23 = (f32[128,256]{1,0:T(8,128)S(1)}, f32[128,256]{1,0:T(8,128)}, u32[]{:S(2)}) copy-start(f32[128,256]{1,0:T(8,128)} %get-tuple-element.312) | copy-start | bytes 393220
  192.1 16.9 %copy-start.27 = (f32[128,256]{1,0:T(8,128)S(1)}, f32[128,256]{1,0:T(8,128)}, u32[]{:S(2)}) copy-start(f32[128,256]{1,0:T(8,128)} %get-tuple-element.314) | copy-start | bytes 393220
  192.2 16.9 %copy-start.31 = (f32[128,256]{1,0:T(8,128)S(1)}, f32[128,256]{1,0:T(8,128)}, u32[]{:S(2)}) copy-start(f32[128,256]{1,0:T(8,128)} %get-tuple-element.315) | copy-start | bytes 393220
  211.5 97.8 %reduce-scatter.14.cloned.1.call-start = ((), (), s32[]{:S(2)}) async-start(), calls=%async_computation.9 | async-start | bytes 884736 | tf_op jit(solution)/shard_map/reduce_scatter | solution.py:71
  248.3 6.8 %collective-permute-start.2 = (f32[3,32,256]{2,1,0:T(8,128)}, f32[3,32,256]{2,1,0:T(8,128)}, u32[]{:S(2)}, u32[]{:S(2)}) collective-permute-start(f32[3,32,256]{2,1,0:T(8,128)} %fusion.82), channel_id=1, source_target_pairs={{8,0},{16,8},{24,16},{9,1},{17,9},{25,17},{10,2},{18,10},{26,18},{... | collective-permute-start | bytes 294920 | tf_op jit(solution)/shard_map/ppermute | solution.py:13
  255.1 17.9 %copy-start.36 = (f32[128,256]{1,0:T(8,128)S(1)}, f32[128,256]{1,0:T(8,128)}, u32[]{:S(2)}) copy-start(f32[128,256]{1,0:T(8,128)} %get-tuple-element.291) | copy-start | bytes 393220
  256.2 16.9 %copy-start.24 = (f32[128,256]{1,0:T(8,128)S(1)}, f32[128,256]{1,0:T(8,128)}, u32[]{:S(2)}) copy-start(f32[128,256]{1,0:T(8,128)} %get-tuple-element.312) | copy-start | bytes 393220
  256.2 16.9 %copy-start.28 = (f32[128,256]{1,0:T(8,128)S(1)}, f32[128,256]{1,0:T(8,128)}, u32[]{:S(2)}) copy-start(f32[128,256]{1,0:T(8,128)} %get-tuple-element.314) | copy-start | bytes 393220
  256.2 16.9 %copy-start.32 = (f32[128,256]{1,0:T(8,128)S(1)}, f32[128,256]{1,0:T(8,128)}, u32[]{:S(2)}) copy-start(f32[128,256]{1,0:T(8,128)} %get-tuple-element.315) | copy-start | bytes 393220
  (29 other events, 310.8 us)
Sparse Core Ops, SparseCore 0:
  30.6 33.0 reduce-scatter.5
  84.0 34.8 reduce-scatter.7
  148.2 34.3 reduce-scatter.9
  211.6 34.9 reduce-scatter.11
  280.4 28.8 reduce-scatter.13
where the time goes:
time: 318 us
  waiting for transfers between devices  174 us (55%)
  blocking collectives  80.7 us (25%)
  other arithmetic  22.3 us (7%)
  between operations  14.5 us (5%)
  matrix products  12.5 us (4%)
  local copies, waits for them, and re-layouts  8.76 us (3%)
  starting transfers between devices  4.04 us (1%)
    reduce_scatter x4, waiting for transfers between devices, per_device(): lax.psum_scatter(second_state + apply_state, 'tok', scatter_dimension=1,...  128 us
    all_gather x4, blocking collectives, per_device(): d_grad = lax.all_gather(-d_shifted, 'tok', axis=1, tiled=True)  63.2 us
    reduce_scatter x1, waiting for transfers between devices, per_device(): lax.psum_scatter(grad_part, 'tok', scatter_dimension=1, tiled=True)  29.1 us
    all_gather x1, blocking collectives, per_device(): gathered = lax.all_gather(own_rows, 'tok', axis=1, tiled=True)  17.5 us
    ppermute x3, waiting for transfers between devices, from_behind(): return lax.ppermute(array, axis, pairs)  16.6 us
  transfers between devices with their start and end apart: 8, of which 8 were waited for; matrix products, arithmetic and copies ran while one was open for 2% of the time, Pallas kernels for 0%

commit v1 on v0

--- a/solution.py
+++ b/solution.py
@@ -64,7 +64,25 @@
     for section in range(groups):
         active = position == groups - 1 - section
         d_shifted, direct = norm_adjoint(incoming, shifted, own_rows, row_norm, new_norm)
-        d_grad = lax.all_gather(-d_shifted, "tok", axis=1, tiled=True)
+        array_2 = -d_shifted
+        ways, here, step = (lax.axis_size("tok"), lax.axis_index("tok"), array_2.shape[1])
+        shape = [n * ways if d == 1 else n for d, n in enumerate(array_2.shape)]
+        d_grad = lax.dynamic_update_slice_in_dim(
+            jnp.zeros(shape, array_2.dtype), array_2, here * step, axis=1
+        )
+        going_up = going_down = array_2
+        for far in range(1, ways // 2 + 1):
+            going_up = lax.ppermute(going_up, "tok", [(d, (d + 1) % ways) for d in range(ways)])
+            d_grad = lax.dynamic_update_slice_in_dim(
+                d_grad, going_up, (here - far) % ways * step, axis=1
+            )
+            if 2 * far < ways:
+                going_down = lax.ppermute(
+                    going_down, "tok", [(d, (d - 1) % ways) for d in range(ways)]
+                )
+                d_grad = lax.dynamic_update_slice_in_dim(
+                    d_grad, going_down, (here + far) % ways * step, axis=1
+                )
         second_state, second_keys, second_values, second_rates = lax.cond(
             active, lambda cot: second_back(cot), lambda cot: zero_back, d_grad
         )

time: 318 us -> 436 us (1.37)
  waiting for transfers between devices: 174 us -> 290 us
  blocking collectives: 80.7 us -> 17.5 us
  starting transfers between devices: 4.04 us -> 41.1 us
  local copies, waits for them, and re-layouts: 8.76 us -> 39 us
    all_gather x4 -> x0, blocking collectives: 63.2 us -> none  [per_device(): d_grad = lax.all_gather(-d_shifted, 'tok', axis=1, tiled=True)]
    reduce_scatter x4, waiting for transfers between devices: 128 us -> 192 us  [per_device(): lax.psum_scatter(second_state + apply_state, 'tok', scatter_dimension=1,...]
    ppermute x0 -> x28, waiting for transfers between devices: none -> 51.3 us  [the longest x16 50.4 us: per_device(): lax.ppermute(going_up, 'tok', [(d, (d + 1) % ways) for d in range(ways)])]
    ppermute x0 -> x28, starting transfers between devices: none -> 37 us  [the longest x12 36.8 us: per_device(): lax.ppermute(going_down, 'tok', [(d, (d - 1) % ways) for d in range(ways)])]
    another operation x9 -> x22, local copies, waits for them, and re-layouts: 3.94 us -> 14.6 us
    dynamic_update_slice x0 -> x8, local copies, waits for them, and re-layouts: none -> 9.11 us  [the longest x4 4.53 us: per_device(): lax.dynamic_update_slice_in_dim(d_grad, going_up, (here - far) % ways * s...]
    unnamed x90 -> x140, local copies, waits for them, and re-layouts: 3.79 us -> 10.8 us
  transfers between devices with their start and end apart: 8 -> 36, of which waited for: 8 -> 27; matrix products, arithmetic and copies ran while one was open for 2% -> 2% of each run, Pallas kernels for 0% -> 0%
where the time goes in v1:
time: 436 us; the launch traced here: 435 us
  waiting for transfers between devices  290 us (67%)
  starting transfers between devices  41.1 us (9%)
  local copies, waits for them, and re-layouts  39 us (9%)
  other arithmetic  18.6 us (4%)
  blocking collectives  17.5 us (4%)
  between operations  14.6 us (3%)
  matrix products  13.3 us (3%)
    reduce_scatter x4, waiting for transfers between devices, per_device(): lax.psum_scatter(second_state + apply_state, 'tok', scatter_dimension=1,...  192 us
    ppermute x16, waiting for transfers between devices, per_device(): lax.ppermute(going_up, 'tok', [(d, (d + 1) % ways) for d in range(ways)])  50.4 us
    ppermute x12, starting transfers between devices, per_device(): lax.ppermute(going_down, 'tok', [(d, (d - 1) % ways) for d in range(ways)])  36.8 us
    reduce_scatter x1, waiting for transfers between devices, per_device(): lax.psum_scatter(grad_part, 'tok', scatter_dimension=1, tiled=True)  31.7 us
    all_gather x1, blocking collectives, per_device(): gathered = lax.all_gather(own_rows, 'tok', axis=1, tiled=True)  17.5 us
    ppermute x3, waiting for transfers between devices, from_behind(): return lax.ppermute(array, axis, pairs)  15.6 us
    another operation x22, local copies, waits for them, and re-layouts  14.6 us
    unnamed x140, local copies, waits for them, and re-layouts  10.8 us
  transfers between devices with their start and end apart: 36, of which 27 were waited for; matrix products, arithmetic and copies ran while one was open for 2% of the time, Pallas kernels for 0%

profile of v1, /device:TPU:0, one launch (start us, length us, event | category | flops | bytes accessed | tf_op | source)
XLA Modules:
  0.0 435.1 jit_solution(9383541837243958455)
XLA Ops:
  7.9 17.5 %all-gather = f32[1,3,256,256]{3,2,1,0:T(8,128)S(1)} all-gather(f32[1,3,32,256]{3,2,1,0:T(8,128)} %param.19), channel_id=2, replica_groups=mesh['block'=4,'tok'=8] {'tok'}, dimensions={2}, use_global_device_ids=true | all-gather | bytes 884736 | tf_op jit(solution)/shard_map/all_gather | solution.py:45
  32.2 31.7 %reduce-scatter.6.cloned.1.call-done = f32[3,32,256]{2,1,0:T(8,128)} async-done(((f32[3,256,256]{2,1,0:T(8,128)}), f32[3,32,256]{2,1,0:T(8,128)}) %reduce-scatter.6.cloned.1.call-update) | async-done | bytes 98320 | tf_op jit(solution)/shard_map/reduce_scatter | solution.py:49
  71.8 3.4 collective-permute-start.3
  77.6 3.6 collective-permute-start.5
  83.4 5.4 %collective-permute-done.6 = f32[3,32,256]{2,1,0:T(8,128)S(1)} collective-permute-done((f32[3,32,256]{2,1,0:T(8,128)S(1)}, f32[3,32,256]{2,1,0:T(8,128)S(1)}, u32[]{:S(2)}, u32[]{:S(2)}) %collective-permute-start.6) | collective-permute-done | bytes 98336 | tf_op jit(solution)/shard_map/ppermute | solution.py:75
  94.0 56.8 %reduce-scatter.8.cloned.1.call-done = f32[3,32,256]{2,1,0:T(8,128)} async-done(((f32[3,256,256]{2,1,0:T(8,128)}), f32[3,32,256]{2,1,0:T(8,128)}) %reduce-scatter.8.cloned.1.call-update) | async-done | bytes 98320 | tf_op jit(solution)/shard_map/reduce_scatter | solution.py:89
  153.1 5.2 %collective-permute-done.7 = f32[3,32,256]{2,1,0:T(8,128)S(1)} collective-permute-done((f32[3,32,256]{2,1,0:T(8,128)S(1)}, f32[3,32,256]{2,1,0:T(8,128)S(1)}, u32[]{:S(2)}, u32[]{:S(2)}) %collective-permute-start.7) | collective-permute-done | bytes 98336 | tf_op jit(solution)/shard_map/ppermute | solution.py:13
  159.7 3.0 collective-permute-start.9
  166.0 2.9 collective-permute-start.11
  172.0 3.1 collective-permute-start.13
  177.6 5.9 %collective-permute-done.14 = f32[3,32,256]{2,1,0:T(8,128)} collective-permute-done((f32[3,32,256]{2,1,0:T(8,128)}, f32[3,32,256]{2,1,0:T(8,128)}, u32[]{:S(2)}, u32[]{:S(2)}) %collective-permute-start.14) | collective-permute-done | bytes 98336 | tf_op jit(solution)/shard_map/ppermute | solution.py:75
  188.0 55.6 %reduce-scatter.10.cloned.1.call-done = f32[3,32,256]{2,1,0:T(8,128)} async-done(((f32[3,256,256]{2,1,0:T(8,128)}), f32[3,32,256]{2,1,0:T(8,128)}) %reduce-scatter.10.cloned.1.call-update) | async-done | bytes 98320 | tf_op jit(solution)/shard_map/reduce_scatter | solution.py:89
  246.0 5.2 %collective-permute-done.15 = f32[3,32,256]{2,1,0:T(8,128)S(1)} collective-permute-done((f32[3,32,256]{2,1,0:T(8,128)S(1)}, f32[3,32,256]{2,1,0:T(8,128)S(1)}, u32[]{:S(2)}, u32[]{:S(2)}) %collective-permute-start.15) | collective-permute-done | bytes 98336 | tf_op jit(solution)/shard_map/ppermute | solution.py:13
  252.7 3.0 collective-permute-start.17
  259.0 2.9 collective-permute-start.19
  265.0 3.0 collective-permute-start.21
  270.5 5.9 %collective-permute-done.22 = f32[3,32,256]{2,1,0:T(8,128)} collective-permute-done((f32[3,32,256]{2,1,0:T(8,128)}, f32[3,32,256]{2,1,0:T(8,128)}, u32[]{:S(2)}, u32[]{:S(2)}) %collective-permute-start.22) | collective-permute-done | bytes 98336 | tf_op jit(solution)/shard_map/ppermute | solution.py:75
  281.0 56.4 %reduce-scatter.12.cloned.1.call-done = f32[3,32,256]{2,1,0:T(8,128)} async-done(((f32[3,256,256]{2,1,0:T(8,128)}), f32[3,32,256]{2,1,0:T(8,128)}) %reduce-scatter.12.cloned.1.call-update) | async-done | bytes 98320 | tf_op jit(solution)/shard_map/reduce_scatter | solution.py:89
  339.8 5.2 %collective-permute-done.23 = f32[3,32,256]{2,1,0:T(8,128)S(1)} collective-permute-done((f32[3,32,256]{2,1,0:T(8,128)S(1)}, f32[3,32,256]{2,1,0:T(8,128)S(1)}, u32[]{:S(2)}, u32[]{:S(2)}) %collective-permute-start.23) | collective-permute-done | bytes 98336 | tf_op jit(solution)/shard_map/ppermute | solution.py:13
  346.4 3.0 collective-permute-start.25
  358.7 3.0 collective-permute-start.29
  364.2 5.9 %collective-permute-done.30 = f32[3,32,256]{2,1,0:T(8,128)} collective-permute-done((f32[3,32,256]{2,1,0:T(8,128)}, f32[3,32,256]{2,1,0:T(8,128)}, u32[]{:S(2)}, u32[]{:S(2)}) %collective-permute-start.30) | collective-permute-done | bytes 98336 | tf_op jit(solution)/shard_map/ppermute | solution.py:75
  370.2 27.8 %conditional.7 = (f32[3,256,256]{2,1,0:T(8,128)S(1)}, f32[128,256]{1,0:T(8,128)}, f32[128]{0:T(128)S(1)}, f32[128,256]{1,0:T(8,128)S(1)}) conditional(s32[]{:T(128)} %convert_element_type.12, () %tuple.67, (f32[3,32,256]{2,1,0:T(8,128)}, s32[]{:T(128)}, f32[3,32,256]{2,1,0:T(8,128)}, s32[]{:T(128)}, f32[3,32,256]{2,1,0:T(8,128)}, ...), branch_computations={%region_19.20_spmd, %region_20.22_spmd} | conditional | flops 1209499520 | bytes 25822780 | solution.py:86
  404.2 22.7 %reduce-scatter.14.cloned.1.call-done = f32[3,32,256]{2,1,0:T(8,128)} async-done(((f32[3,256,256]{2,1,0:T(8,128)}), f32[3,32,256]{2,1,0:T(8,128)}) %reduce-scatter.14.cloned.1.call-update) | async-done | bytes 98320 | tf_op jit(solution)/shard_map/reduce_scatter | solution.py:89
  (319 shorter events, 116.3 us)
Async XLA Ops:
  7.2 56.8 %reduce-scatter.6.cloned.1.call-start = ((), (), s32[]{:S(2)}) async-start(), calls=%async_computation.5 | async-start | bytes 884736 | tf_op jit(solution)/shard_map/reduce_scatter | solution.py:49
  30.8 119.9 %reduce-scatter.8.cloned.1.call-start = ((), (), s32[]{:S(2)}) async-start(), calls=%async_computation.6 | async-start | bytes 884736 | tf_op jit(solution)/shard_map/reduce_scatter | solution.py:89
  65.1 6.0 %collective-permute-start = (f32[3,32,256]{2,1,0:T(8,128)S(1)}, f32[3,32,256]{2,1,0:T(8,128)S(1)}, u32[]{:S(2)}, u32[]{:S(2)}) collective-permute-start(f32[3,32,256]{2,1,0:T(8,128)S(1)} %fusion.40), channel_id=1, source_target_pairs={{0,1},{1,2},{2,3},{3,4},{4,5},{5,6},{6,7},{7,0},{8,9},{9,10},{10,1... | collective-permute-start | bytes 294920 | tf_op jit(solution)/shard_map/ppermute | solution.py:75
  71.1 6.0 %collective-permute-start.2 = (f32[3,32,256]{2,1,0:T(8,128)S(1)}, f32[3,32,256]{2,1,0:T(8,128)S(1)}, u32[]{:S(2)}, u32[]{:S(2)}) collective-permute-start(f32[3,32,256]{2,1,0:T(8,128)S(1)} %collective-permute-done), channel_id=1, source_target_pairs={{0,1},{1,2},{2,3},{3,4},{4,5},{5,6},{6,7},{7,0},{8,9},{9,10},{10,1... | collective-permute-start | bytes 294920 | tf_op jit(solution)/shard_map/ppermute | solution.py:75
  77.1 5.8 %collective-permute-start.4 = (f32[3,32,256]{2,1,0:T(8,128)S(1)}, f32[3,32,256]{2,1,0:T(8,128)S(1)}, u32[]{:S(2)}, u32[]{:S(2)}) collective-permute-start(f32[3,32,256]{2,1,0:T(8,128)S(1)} %collective-permute-done.2), channel_id=1, source_target_pairs={{0,1},{1,2},{2,3},{3,4},{4,5},{5,6},{6,7},{7,0},{8,9},{9,10},{10,1... | collective-permute-start | bytes 294920 | tf_op jit(solution)/shard_map/ppermute | solution.py:75
  83.0 5.8 %collective-permute-start.6 = (f32[3,32,256]{2,1,0:T(8,128)S(1)}, f32[3,32,256]{2,1,0:T(8,128)S(1)}, u32[]{:S(2)}, u32[]{:S(2)}) collective-permute-start(f32[3,32,256]{2,1,0:T(8,128)S(1)} %collective-permute-done.4), channel_id=1, source_target_pairs={{0,1},{1,2},{2,3},{3,4},{4,5},{5,6},{6,7},{7,0},{8,9},{9,10},{10,1... | collective-permute-start | bytes 294920 | tf_op jit(solution)/shard_map/ppermute | solution.py:75
  93.9 149.7 %reduce-scatter.10.cloned.1.call-start = ((), (), s32[]{:S(2)}) async-start(), calls=%async_computation.7 | async-start | bytes 884736 | tf_op jit(solution)/shard_map/reduce_scatter | solution.py:89
  151.8 6.5 %collective-permute-start.7 = (f32[3,32,256]{2,1,0:T(8,128)S(1)}, f32[3,32,256]{2,1,0:T(8,128)S(1)}, u32[]{:S(2)}, u32[]{:S(2)}) collective-permute-start(f32[3,32,256]{2,1,0:T(8,128)S(1)} %fusion.24), channel_id=1, source_target_pairs={{8,0},{16,8},{24,16},{9,1},{17,9},{25,17},{10,2},{18,10},{26,18},{... | collective-permute-start | bytes 294920 | tf_op jit(solution)/shard_map/ppermute | solution.py:13
  159.1 6.3 %collective-permute-start.8 = (f32[3,32,256]{2,1,0:T(8,128)S(1)}, f32[3,32,256]{2,1,0:T(8,128)S(1)}, u32[]{:S(2)}, u32[]{:S(2)}) collective-permute-start(f32[3,32,256]{2,1,0:T(8,128)S(1)} %fusion.41), channel_id=1, source_target_pairs={{0,1},{1,2},{2,3},{3,4},{4,5},{5,6},{6,7},{7,0},{8,9},{9,10},{10,1... | collective-permute-start | bytes 294920 | tf_op jit(solution)/shard_map/ppermute | solution.py:75
  165.4 6.0 %collective-permute-start.10 = (f32[3,32,256]{2,1,0:T(8,128)S(1)}, f32[3,32,256]{2,1,0:T(8,128)S(1)}, u32[]{:S(2)}, u32[]{:S(2)}) collective-permute-start(f32[3,32,256]{2,1,0:T(8,128)S(1)} %collective-permute-done.8), channel_id=1, source_target_pairs={{0,1},{1,2},{2,3},{3,4},{4,5},{5,6},{6,7},{7,0},{8,9},{9,10},{10,1... | collective-permute-start | bytes 294920 | tf_op jit(solution)/shard_map/ppermute | solution.py:75
  171.4 5.9 %collective-permute-start.12 = (f32[3,32,256]{2,1,0:T(8,128)S(1)}, f32[3,32,256]{2,1,0:T(8,128)}, u32[]{:S(2)}, u32[]{:S(2)}) collective-permute-start(f32[3,32,256]{2,1,0:T(8,128)S(1)} %collective-permute-done.10), channel_id=1, source_target_pairs={{0,1},{1,2},{2,3},{3,4},{4,5},{5,6},{6,7},{7,0},{8,9},{9,10},{10,1... | collective-permute-start | bytes 294920 | tf_op jit(solution)/shard_map/ppermute | solution.py:75
  177.3 6.2 %collective-permute-start.14 = (f32[3,32,256]{2,1,0:T(8,128)}, f32[3,32,256]{2,1,0:T(8,128)}, u32[]{:S(2)}, u32[]{:S(2)}) collective-permute-start(f32[3,32,256]{2,1,0:T(8,128)} %collective-permute-done.12), channel_id=1, source_target_pairs={{0,1},{1,2},{2,3},{3,4},{4,5},{5,6},{6,7},{7,0},{8,9},{9,10},{10,1... | collective-permute-start | bytes 294920 | tf_op jit(solution)/shard_map/ppermute | solution.py:75
  188.0 149.4 %reduce-scatter.12.cloned.1.call-start = ((), (), s32[]{:S(2)}) async-start(), calls=%async_computation.8 | async-start | bytes 884736 | tf_op jit(solution)/shard_map/reduce_scatter | solution.py:89
  244.7 6.5 %collective-permute-start.15 = (f32[3,32,256]{2,1,0:T(8,128)S(1)}, f32[3,32,256]{2,1,0:T(8,128)S(1)}, u32[]{:S(2)}, u32[]{:S(2)}) collective-permute-start(f32[3,32,256]{2,1,0:T(8,128)S(1)} %fusion.27), channel_id=1, source_target_pairs={{8,0},{16,8},{24,16},{9,1},{17,9},{25,17},{10,2},{18,10},{26,18},{... | collective-permute-start | bytes 294920 | tf_op jit(solution)/shard_map/ppermute | solution.py:13
  252.0 6.3 %collective-permute-start.16 = (f32[3,32,256]{2,1,0:T(8,128)S(1)}, f32[3,32,256]{2,1,0:T(8,128)S(1)}, u32[]{:S(2)}, u32[]{:S(2)}) collective-permute-start(f32[3,32,256]{2,1,0:T(8,128)S(1)} %fusion.42), channel_id=1, source_target_pairs={{0,1},{1,2},{2,3},{3,4},{4,5},{5,6},{6,7},{7,0},{8,9},{9,10},{10,1... | collective-permute-start | bytes 294920 | tf_op jit(solution)/shard_map/ppermute | solution.py:75
  258.3 6.0 %collective-permute-start.18 = (f32[3,32,256]{2,1,0:T(8,128)S(1)}, f32[3,32,256]{2,1,0:T(8,128)S(1)}, u32[]{:S(2)}, u32[]{:S(2)}) collective-permute-start(f32[3,32,256]{2,1,0:T(8,128)S(1)} %collective-permute-done.16), channel_id=1, source_target_pairs={{0,1},{1,2},{2,3},{3,4},{4,5},{5,6},{6,7},{7,0},{8,9},{9,10},{10,1... | collective-permute-start | bytes 294920 | tf_op jit(solution)/shard_map/ppermute | solution.py:75
  264.3 5.9 %collective-permute-start.20 = (f32[3,32,256]{2,1,0:T(8,128)S(1)}, f32[3,32,256]{2,1,0:T(8,128)}, u32[]{:S(2)}, u32[]{:S(2)}) collective-permute-start(f32[3,32,256]{2,1,0:T(8,128)S(1)} %collective-permute-done.18), channel_id=1, source_target_pairs={{0,1},{1,2},{2,3},{3,4},{4,5},{5,6},{6,7},{7,0},{8,9},{9,10},{10,1... | collective-permute-start | bytes 294920 | tf_op jit(solution)/shard_map/ppermute | solution.py:75
  270.3 6.2 %collective-permute-start.22 = (f32[3,32,256]{2,1,0:T(8,128)}, f32[3,32,256]{2,1,0:T(8,128)}, u32[]{:S(2)}, u32[]{:S(2)}) collective-permute-start(f32[3,32,256]{2,1,0:T(8,128)} %collective-permute-done.20), channel_id=1, source_target_pairs={{0,1},{1,2},{2,3},{3,4},{4,5},{5,6},{6,7},{7,0},{8,9},{9,10},{10,1... | collective-permute-start | bytes 294920 | tf_op jit(solution)/shard_map/ppermute | solution.py:75
  280.9 146.0 %reduce-scatter.14.cloned.1.call-start = ((), (), s32[]{:S(2)}) async-start(), calls=%async_computation.9 | async-start | bytes 884736 | tf_op jit(solution)/shard_map/reduce_scatter | solution.py:89
  338.5 6.5 %collective-permute-start.23 = (f32[3,32,256]{2,1,0:T(8,128)S(1)}, f32[3,32,256]{2,1,0:T(8,128)S(1)}, u32[]{:S(2)}, u32[]{:S(2)}) collective-permute-start(f32[3,32,256]{2,1,0:T(8,128)S(1)} %fusion.30), channel_id=1, source_target_pairs={{8,0},{16,8},{24,16},{9,1},{17,9},{25,17},{10,2},{18,10},{26,18},{... | collective-permute-start | bytes 294920 | tf_op jit(solution)/shard_map/ppermute | solution.py:13
  345.8 6.3 %collective-permute-start.24 = (f32[3,32,256]{2,1,0:T(8,128)S(1)}, f32[3,32,256]{2,1,0:T(8,128)S(1)}, u32[]{:S(2)}, u32[]{:S(2)}) collective-permute-start(f32[3,32,256]{2,1,0:T(8,128)S(1)} %fusion.43), channel_id=1, source_target_pairs={{0,1},{1,2},{2,3},{3,4},{4,5},{5,6},{6,7},{7,0},{8,9},{9,10},{10,1... | collective-permute-start | bytes 294920 | tf_op jit(solution)/shard_map/ppermute | solution.py:75
  352.0 6.0 %collective-permute-start.26 = (f32[3,32,256]{2,1,0:T(8,128)S(1)}, f32[3,32,256]{2,1,0:T(8,128)S(1)}, u32[]{:S(2)}, u32[]{:S(2)}) collective-permute-start(f32[3,32,256]{2,1,0:T(8,128)S(1)} %collective-permute-done.24), channel_id=1, source_target_pairs={{0,1},{1,2},{2,3},{3,4},{4,5},{5,6},{6,7},{7,0},{8,9},{9,10},{10,1... | collective-permute-start | bytes 294920 | tf_op jit(solution)/shard_map/ppermute | solution.py:75
  358.0 5.9 %collective-permute-start.28 = (f32[3,32,256]{2,1,0:T(8,128)S(1)}, f32[3,32,256]{2,1,0:T(8,128)}, u32[]{:S(2)}, u32[]{:S(2)}) collective-permute-start(f32[3,32,256]{2,1,0:T(8,128)S(1)} %collective-permute-done.26), channel_id=1, source_target_pairs={{0,1},{1,2},{2,3},{3,4},{4,5},{5,6},{6,7},{7,0},{8,9},{9,10},{10,1... | collective-permute-start | bytes 294920 | tf_op jit(solution)/shard_map/ppermute | solution.py:75
  364.0 6.2 %collective-permute-start.30 = (f32[3,32,256]{2,1,0:T(8,128)}, f32[3,32,256]{2,1,0:T(8,128)}, u32[]{:S(2)}, u32[]{:S(2)}) collective-permute-start(f32[3,32,256]{2,1,0:T(8,128)} %collective-permute-done.28), channel_id=1, source_target_pairs={{0,1},{1,2},{2,3},{3,4},{4,5},{5,6},{6,7},{7,0},{8,9},{9,10},{10,1... | collective-permute-start | bytes 294920 | tf_op jit(solution)/shard_map/ppermute | solution.py:75
  (100 other events, 1655.7 us)
Sparse Core Ops, SparseCore 0:
  30.9 33.0 reduce-scatter.5
  94.0 56.6 reduce-scatter.7
  188.1 55.4 reduce-scatter.9
  281.1 56.3 reduce-scatter.11
  399.1 27.7 reduce-scatter.13
